TPU v7x, 128 devices: a whole 4x4x4 slice. The times are simulated.
128 devices in a mesh: dev: 16 (over z_hi, y, core), ha: 8 (over z_lo, x).
Axes of the slice: x: 4, y: 4, z: 4 (z_hi: 2, z_lo: 2; z = z_hi * 2 + z_lo), core: 2. Of those that a mesh axis runs over, the one named last changes fastest.
Arguments:
- volume: bfloat16 [4, 128, 128, 512], P(None, 'dev', 'ha'), may hold values from -6 to 6
- w_first: bfloat16 [3, 3, 3, 4, 32], replicated, may hold values from -0.625 to 0.625
- w_second: bfloat16 [3, 3, 3, 32, 64], replicated, may hold values from -0.21875 to 0.21875
- w_third: bfloat16 [3, 3, 3, 64, 128], P(None, None, None, None, 'ha'), may hold values from -0.15625 to 0.15625
- cotangent: bfloat16 [128, 16, 16, 64], P('ha', 'dev'), may hold values from -6 to 6
Outputs:
- out_third: bfloat16 [128, 16, 16, 64], P('ha', 'dev')
- grad_first: float32 [3, 3, 3, 4, 32], replicated
- grad_second: float32 [3, 3, 3, 32, 64], replicated
- grad_third: float32 [3, 3, 3, 64, 128], P(None, None, None, None, 'ha')
All inputs are finite; a program needn't handle non-finite values.
Results may differ from a plain program's by a relative error of at most 0.0063.
Values may be sent and summed in bfloat16 or wider, within the bound.
A program may use at most 192 MiB of HBM per device.

v0:
```python
import math
import jax
import jax.numpy as jnp
from jax import lax
from jax.sharding import PartitionSpec as P


def shifted(block, axis, distance):
    devices = range(lax.axis_size(axis))
    route = [(i - distance, i) for i in devices if i - distance in devices]
    return lax.ppermute(block, axis, route)


def leaky_relu(values):
    return 0.3 * values + 0.175 * jax.nn.softplus(4.0 * values)


def leaky_slope(values):
    return 0.3 + 0.7 * jax.nn.sigmoid(4.0 * values)


def convolve(inputs, kernel, pad_depth, pad_height):
    return lax.conv_general_dilated(
        inputs[None],
        kernel,
        (2, 2, 2),
        [pad_depth, pad_height, (1, 0)],
        dimension_numbers=("NCDHW", "DHWIO", "NCDHW"),
        preferred_element_type=jnp.float32,
    )[0]


def weight_grad(inputs, delta, pad_depth, pad_height):
    result = lax.conv_general_dilated(
        inputs[:, None],
        delta[:, None],
        (1, 1, 1),
        [pad_depth, pad_height, (1, 0)],
        rhs_dilation=(2, 2, 2),
        dimension_numbers=("NCDHW", "OIDHW", "NCDHW"),
        preferred_element_type=jnp.float32,
    )
    return jnp.transpose(result, (2, 3, 4, 0, 1))


def input_grad(delta, kernel):
    flipped = jnp.flip(kernel, (0, 1, 2))
    return lax.conv_general_dilated(
        delta[None],
        flipped,
        (1, 1, 1),
        [(2, 2)] * 3,
        lhs_dilation=(2, 2, 2),
        dimension_numbers=("NCDHW", "DHWOI", "NCDHW"),
        preferred_element_type=jnp.float32,
    )[0]


def extend_depth(values):
    lower = shifted(values[:, -1:], "dev", 1)
    return jnp.concatenate([lower, values], 1)


def extend(values):
    deeper = extend_depth(values)
    beside = shifted(deeper[:, :, -1:], "ha", 1)
    return jnp.concatenate([beside, deeper], 2)


def retract_depth(grads):
    lower = shifted(grads[:, 0:1], "dev", -1)
    inner = grads[:, 1:]
    return inner.at[:, -1:].add(lower)


def retract(grads):
    beside = shifted(grads[:, :, 0:1].astype(jnp.bfloat16), "ha", -1).astype(jnp.float32)
    inner = grads[:, :, 1:]
    inner = inner.at[:, :, -1:].add(beside)
    return retract_depth(inner)


def local(volume, w_first, w_second, w_third, cotangent):
    depth_total = volume.shape[1] * lax.axis_size("dev")
    height_total = volume.shape[2] * lax.axis_size("ha")
    width_total = volume.shape[3]
    scale_first = 1.0 / math.sqrt(depth_total // 2 * (height_total // 2) * (width_total // 2))
    scale_second = 1.0 / math.sqrt(depth_total // 4 * (height_total // 4) * (width_total // 4))
    scale_third = 1.0 / math.sqrt(depth_total // 8 * (height_total // 8) * (width_total // 8))
    whole_first = extend(volume)
    pre_first = convolve(whole_first, w_first, (0, 0), (0, 0))
    act_first = leaky_relu(pre_first).astype(jnp.bfloat16)
    whole_second = extend(act_first)
    pre_second = convolve(whole_second, w_second, (0, 0), (0, 0))
    act_second = leaky_relu(pre_second).astype(jnp.bfloat16)
    deeper = extend_depth(act_second)
    all_rows = lax.all_gather(deeper, "ha", axis=2, tiled=True)
    pre_third = convolve(all_rows, w_third, (0, 0), (1, 0))
    out_third = leaky_relu(pre_third).astype(jnp.bfloat16)
    delta_third = (cotangent.astype(jnp.float32) * leaky_slope(pre_third)).astype(jnp.bfloat16)
    grad_third = lax.psum(weight_grad(all_rows, delta_third, (0, 0), (1, 0)), "dev") * scale_third
    partial_back = input_grad(delta_third, w_third)[:, :, 1:, 1:]
    summed_back = lax.psum_scatter(partial_back, "ha", scatter_dimension=2, tiled=True)
    back_second = retract_depth(summed_back)
    delta_second = (back_second * leaky_slope(pre_second)).astype(jnp.bfloat16)
    local_second = weight_grad(whole_second, delta_second, (0, 0), (0, 0))
    back_first = retract(input_grad(delta_second, w_second)[..., 1:])
    delta_first = (back_first * leaky_slope(pre_first)).astype(jnp.bfloat16)
    local_first = weight_grad(whole_first, delta_first, (0, 0), (0, 0))
    grad_first, grad_second = lax.psum((local_first, local_second), ("dev", "ha"))
    return (out_third, grad_first * scale_first, grad_second * scale_second, grad_third)


def solution(mesh):
    placed = (
        P(None, "dev", "ha", None),
        P(),
        P(),
        P(None, None, None, None, "ha"),
        P("ha", "dev", None, None),
    )
    return jax.shard_map(
        local,
        mesh=mesh,
        in_specs=placed,
        out_specs=(P("ha", "dev", None, None), P(), P(), P(None, None, None, None, "ha")),
        check_vma=False,
    )
```

profile of v0, /device:TPU:1, one launch (start us, length us, event | category | flops | bytes accessed | tf_op | source)
XLA Modules:
  0.0 800.9 jit_solution(4794022419760191605)
XLA Ops:
  8.1 4.6 collective-permute-start
  22.9 10.8 %copy.123 = bf16[4,9,17,1,8,66]{4,0,5,2,1,3:T(4,128)(2,1)} copy(bf16[4,9,17,1,8,66]{5,4,2,1,0,3:T(8,128)(2,1)S(1)} %reshape.287) | data formatting | bytes 1292544 | tf_op jit(solution)/shard_map/conv_general_dilated | solution.py:23
  35.0 32.7 %fusion.3 = f32[4,8,8,33,32]{4,2,3,1,0:T(8,128)} fusion(bf16[3,3,3,4,32]{4,3,2,1,0:T(4,128)(2,1)S(1)} %copy-done.15, bf16[4,9,17,1,7,2]{4,0,5,2,1,3:T(4,128)(2,1)S(1)} %slice.159, bf16[4,9,17,1,8,66]{4,0,5,2,1,3:T(4,128)(2,1)} %copy.123), kind=kOutput, calls=%fused_computation.4 | convolution fusion | flops 60390144 | bytes 1751664 | tf_op jit(solution)/shard_map/conv_general_dilated | solution.py:23
  67.7 18.2 %copy.124 = f32[4,8,8,33,32]{3,4,2,1,0:T(8,128)} copy(f32[4,8,8,33,32]{4,2,3,1,0:T(8,128)} %fusion.3) | data formatting | bytes 2162688 | tf_op jit(solution)/shard_map/conv_general_dilated | solution.py:23
  85.9 5.1 select_multiply_fusion
  91.0 5.9 copy.126
  100.4 8.6 %copy.125 = f32[4,8,8,33,32]{3,2,4,1,0:T(8,128)} copy(f32[4,8,8,33,32]{3,4,2,1,0:T(8,128)} %get-tuple-element.53) | data formatting | bytes 2162688 | tf_op jit(solution)/shard_map/mul | solution.py:15
  113.2 5.1 collective-permute-start.2
  120.2 4.0 collective-permute-start.3
  128.1 4.0 reshape.229
  132.1 4.5 copy.128
  143.1 5.2 collective-permute-start.4
  151.5 48.0 %all-gather.2.cloned.1.call-done = bf16[64,3,32,128]{3,0,1,2:T(8,128)(2,1)} async-done(((bf16[64,3,4,128]{3,0,1,2:T(8,128)(2,1)}), bf16[64,3,32,128]{3,0,1,2:T(8,128)(2,1)}) %all-gather.2.cloned.1.call-update) | async-done | bytes 1572880 | tf_op jit(solution)/shard_map/all_gather | solution.py:97
  199.5 5.8 copy.132
  212.9 4.3 broadcast_select_fusion
  217.1 5.8 copy.143
  223.0 9.0 %reshape.251 = f32[3,33,1,144,64]{4,3,1,0,2:T(8,128)} reshape(f32[3,33,8,18,64]{4,3,2,1,0:T(8,128)} %copy.143) | data formatting | bytes 7299072 | tf_op jit(solution)/shard_map/conv_general_dilated | solution.py:48
  239.1 6.2 copy.144
  245.3 56.0 %copy.151 = bf16[4,1,9,17,512]{0,1,4,3,2:T(2,128)(2,1)} copy(bf16[4,1,9,17,512]{4,3,2,0,1:T(8,128)(2,1)S(1)} %copy-done.8) | data formatting | bytes 1253376 | tf_op jit(solution)/shard_map/broadcast_in_dim | solution.py:35
  301.3 8.8 %copy.153 = bf16[32,1,5,9,256]{0,1,4,3,2:T(2,128)(2,1)} copy(bf16[32,1,5,9,256]{4,0,3,2,1:T(8,128)(2,1)S(1)} %copy-done.9) | data formatting | bytes 1474560 | tf_op jit(solution)/shard_map/broadcast_in_dim | solution.py:35
  310.6 10.5 %copy.156 = bf16[64,1,3,32,128]{0,1,4,3,2:T(2,128)(2,1)} copy(bf16[64,1,3,32,128]{4,0,2,3,1:T(8,128)(2,1)S(1)} %bitcast.160) | data formatting | bytes 3145728 | tf_op jit(solution)/shard_map/broadcast_in_dim | solution.py:35
  322.3 8.7 %collective-permute-start.5 = (f32[64,1,4,128]{0,2,3,1:T(4,128)S(1)}, f32[64,1,4,128]{0,2,3,1:T(4,128)S(1)}, u32[]{:S(2)}, u32[]{:S(2)}) collective-permute-start(f32[64,1,4,128]{0,2,3,1:T(4,128)S(1)} %copy.168), channel_id=1, source_target_pairs={{8,0},{16,8},{24,16},{32,24},{40,32},{48,40},{56,48},{64,56},{72,6... | collective-permute-start | bytes 393224 | tf_op jit(solution)/shard_map/ppermute | solution.py:11
  331.0 15.7 %fusion.86 = f32[3,3,3,64,16]{3,4,2,1,0:T(8,128)} fusion(bf16[64,1,3,32,128]{0,1,4,3,2:T(2,128)(2,1)} %copy.156, bf16[16,1,1,16,64]{0,1,4,3,2:T(2,128)(2,1)S(1)} %copy.157), kind=kOutput, calls=%fused_computation.117 | convolution fusion | flops 55154688 | bytes 1716224 | tf_op jit(solution)/shard_map/transpose | solution.py:43
  348.5 7.4 broadcast_select_fusion.1
  355.9 8.4 %copy.150 = f32[5,9,8,34,32]{3,2,4,1,0:T(8,128)} copy(f32[5,9,8,34,32]{4,2,3,1,0:T(8,128)} %broadcast_select_fusion.1) | data formatting | bytes 3133440 | tf_op jit(solution)/shard_map/conv_general_dilated | solution.py:48
  364.3 4.2 reshape.258
  371.7 14.7 %fusion.35 = f32[3,3,3,32,64]{4,3,2,1,0:T(8,128)} fusion(bf16[32,1,5,9,256]{0,1,4,3,2:T(2,128)(2,1)} %copy.153, bf16[64,1,2,4,128]{0,3,4,2,1:T(4,128)(2,1)S(1)} %fusion.97), kind=kOutput, calls=%fused_computation.49 | convolution fusion | flops 112951296 | bytes 1089536 | tf_op jit(solution)/shard_map/transpose | solution.py:43
  392.5 88.5 %all-reduce.5.cloned.1.call-done = f32[3,3,3,64,16]{3,4,2,1,0:T(8,128)} async-done(((f32[3,3,3,64,16]{3,4,2,1,0:T(8,128)}), f32[3,3,3,64,16]{3,4,2,1,0:T(8,128)}) %all-reduce.5.cloned.1.call-update) | async-done | bytes 110608 | tf_op jit(solution)/shard_map/psum | solution.py:101
  483.7 146.6 %all-reduce.3.cloned.1.call-done = f32[3,3,3,32,64]{4,3,2,1,0:T(8,128)} async-done(((f32[3,3,3,32,64]{4,3,2,1,0:T(8,128)}), f32[3,3,3,32,64]{4,3,2,1,0:T(8,128)}) %all-reduce.3.cloned.1.call-update) | async-done | bytes 221200 | tf_op jit(solution)/shard_map/psum | solution.py:110
  634.4 7.2 copy.152
  641.7 87.7 %fusion.85 = f32[3,3,3,4,32]{4,3,2,1,0:T(4,128)S(1)} fusion(bf16[4,1,9,17,512]{0,1,4,3,2:T(2,128)(2,1)} %copy.151, bf16[32,1,4,8,256]{0,1,4,3,2:T(2,128)(2,1)} %copy.152), kind=kOutput, calls=%fused_computation.116 | convolution fusion | flops 56549376 | bytes 1164800 | tf_op jit(solution)/shard_map/transpose | solution.py:43
  729.4 63.8 %psum.21 = f32[3,3,3,4,32]{4,3,2,1,0:T(4,128)S(1)} all-reduce(f32[3,3,3,4,32]{4,3,2,1,0:T(4,128)S(1)} %fusion.85), channel_id=1, replica_groups=mesh['dev'=16,'ha'=8] {'dev','ha'}, use_global_device_ids=true, to_apply=%region_1.2 | all-reduce | flops 3456 | bytes 27648 | tf_op jit(solution)/shard_map/psum | solution.py:110
  (120 shorter events, 69.9 us)
Async XLA Ops:
  7.2 130.5 %copy-start = (bf16[3,3,3,32,64]{4,3,2,1,0:T(8,128)(2,1)S(1)}, bf16[3,3,3,32,64]{4,3,2,1,0:T(8,128)(2,1)}, u32[]{:S(2)}) copy-start(bf16[3,3,3,32,64]{4,3,2,1,0:T(8,128)(2,1)} %param.13) | copy-start | bytes 331780
  7.2 192.3 %all-gather.2.cloned.1.call-start = ((), (), s32[]{:S(2)}) async-start(), calls=%async_computation.1 | async-start | bytes 1769472 | tf_op jit(solution)/shard_map/all_gather | solution.py:97
  8.1 5.9 collective-permute-start
  15.2 4.5 collective-permute-start.1
  22.9 12.0 %copy-start.15 = (bf16[3,3,3,4,32]{4,3,2,1,0:T(4,128)(2,1)S(1)}, bf16[3,3,3,4,32]{4,3,2,1,0:T(4,128)(2,1)}, u32[]{:S(2)}) copy-start(bf16[3,3,3,4,32]{4,3,2,1,0:T(4,128)(2,1)} %param.12) | copy-start | bytes 20740
  67.7 18.2 %copy-start.14 = (pred[8,33]{1,0:T(8,128)(4,1)S(1)}, pred[8,33]{1,0:T(8,128)(4,1)}, u32[]{:S(2)}) copy-start(pred[8,33]{1,0:T(8,128)(4,1)} %constant.142) | copy-start | bytes 796
  100.4 12.1 %copy-start.2 = (f32[4,8,1,264,32]{3,4,1,0,2:T(8,128)}, f32[4,8,1,264,32]{3,4,1,0,2:T(8,128)S(1)}, u32[]{:S(2)}) copy-start(f32[4,8,1,264,32]{3,4,1,0,2:T(8,128)S(1)} %reshape.226) | copy-start | bytes 3244036
  113.2 7.1 collective-permute-start.2
  120.2 5.5 collective-permute-start.3
  132.1 5.5 copy-start.16
  141.6 0.8 copy-start.4
  143.1 7.1 collective-permute-start.4
  151.5 169.6 %reduce-scatter.2.cloned.1.call-start = ((), (), s32[]{:S(2)}) async-start(), calls=%async_computation.2 | async-start | bytes 3538944 | tf_op jit(solution)/shard_map/reduce_scatter | solution.py:103
  205.9 2.4 copy-start.10
  205.9 2.4 copy-start.17
  210.6 0.9 copy-start.11
  210.6 2.2 copy-start.13
  239.1 6.3 copy-start.8
  245.3 235.7 %all-reduce.5.cloned.1.call-start = ((), (), s32[]{:S(2)}) async-start(), calls=%async_computation.4 | async-start | bytes 442368 | tf_op jit(solution)/shard_map/psum | solution.py:101
  245.3 56.0 %copy-start.9 = (bf16[32,1,5,9,256]{4,0,3,2,1:T(8,128)(2,1)S(1)}, bf16[32,1,5,9,256]{4,0,3,2,1:T(8,128)(2,1)}, u32[]{:S(2)}) copy-start(bf16[32,1,5,9,256]{4,0,3,2,1:T(8,128)(2,1)} %get-tuple-element.54) | copy-start | bytes 2211844
  301.3 9.2 %copy-start.7 = (bf16[64,3,32,128]{3,0,1,2:T(8,128)(2,1)S(1)}, bf16[64,3,32,128]{3,0,1,2:T(8,128)(2,1)}, u32[]{:S(2)}) copy-start(bf16[64,3,32,128]{3,0,1,2:T(8,128)(2,1)} %all-gather.2.cloned.1.call-done) | copy-start | bytes 4718596
  322.2 24.9 %slice-start = ((f32[64,3,4,128]{3,0,1,2:T(8,128)}), f32[64,2,4,128]{3,0,1,2:T(8,128)S(1)}, s32[]{:S(2)}) async-start(f32[64,3,4,128]{3,0,1,2:T(8,128)} %reduce-scatter.2.cloned.1.call-done), calls=%async_computation.5 | async-start | bytes 524288 | tf_op jit(solution)/shard_map/slice | solution.py:72
  322.3 25.3 %copy-start.5 = (f32[2,4,8,17,64]{4,1,3,2,0:T(4,128)S(1)}, f32[2,4,8,17,64]{4,1,3,2,0:T(4,128)}, u32[]{:S(2)}) copy-start(f32[2,4,8,17,64]{4,1,3,2,0:T(4,128)} %copy-done.4) | copy-start | bytes 835588
  322.3 25.2 %collective-permute-start.5 = (f32[64,1,4,128]{0,2,3,1:T(4,128)S(1)}, f32[64,1,4,128]{0,2,3,1:T(4,128)S(1)}, u32[]{:S(2)}, u32[]{:S(2)}) collective-permute-start(f32[64,1,4,128]{0,2,3,1:T(4,128)S(1)} %copy.168), channel_id=1, source_target_pairs={{8,0},{16,8},{24,16},{32,24},{40,32},{48,40},{56,48},{64,56},{72,6... | collective-permute-start | bytes 393224 | tf_op jit(solution)/shard_map/ppermute | solution.py:11
  346.7 1.7 copy-start.12
  346.8 283.5 %all-reduce.3.cloned.1.call-start = ((), (), s32[]{:S(2)}) async-start(), calls=%async_computation.3 | async-start | bytes 884736 | tf_op jit(solution)/shard_map/psum | solution.py:110
  368.6 1.4 copy-start.6
  370.1 18.3 %collective-permute-start.6 = (bf16[32,5,1,256]{3,0,2,1:T(8,128)(2,1)S(1)}, bf16[32,5,1,256]{3,0,2,1:T(8,128)(2,1)S(1)}, u32[]{:S(2)}, u32[]{:S(2)}) collective-permute-start(bf16[32,5,1,256]{3,0,2,1:T(8,128)(2,1)S(1)} %slice.211), channel_id=1, source_target_pairs={{1,0},{2,1},{3,2},{4,3},{5,4},{6,5},{7,6},{9,8},{10,9},{11,10},{12... | collective-permute-start | bytes 245768 | tf_op jit(solution)/shard_map/ppermute | solution.py:11
  386.3 246.5 %copy-start.3 = (f32[4,8,1,264,32]{3,4,1,0,2:T(8,128)S(1)}, f32[4,8,1,264,32]{3,4,1,0,2:T(8,128)}, u32[]{:S(2)}) copy-start(f32[4,8,1,264,32]{3,4,1,0,2:T(8,128)} %copy-done.2) | copy-start | bytes 3244036
  390.3 241.9 %collective-permute-start.7 = (f32[32,1,8,256]{3,0,2,1:T(8,128)}, f32[32,1,8,256]{3,0,2,1:T(8,128)S(1)}, u32[]{:S(2)}, u32[]{:S(2)}) collective-permute-start(f32[32,1,8,256]{3,0,2,1:T(8,128)} %slice.183), channel_id=1, source_target_pairs={{8,0},{16,8},{24,16},{32,24},{40,32},{48,40},{56,48},{64,56},{72,6... | collective-permute-start | bytes 786440 | tf_op jit(solution)/shard_map/ppermute | solution.py:11
  641.7 152.2 %copy-start.1 = (bf16[3,3,3,32,64]{4,3,2,1,0:T(8,128)(2,1)S(1)}, bf16[3,3,3,32,64]{4,3,2,1,0:T(8,128)(2,1)}, u32[]{:S(2)}) copy-start(bf16[3,3,3,32,64]{4,3,2,1,0:T(8,128)(2,1)} %param.13) | copy-start | bytes 331780
Sparse Core Ops, SparseCore 0:
  151.6 47.8 all-gather.1
  245.4 47.8 reduce-scatter.1
  346.9 134.0 all-reduce.4
  486.2 144.0 all-reduce.2
where the time goes:
time: 810 us; the launch traced here: 801 us
  waiting for transfers between devices  291 us (36%)
  local copies, waits for them, and re-layouts  210 us (26%)
  matrix products  168 us (21%)
  blocking collectives  63.8 us (8%)
  starting transfers between devices  34.9 us (4%)
  other arithmetic  18 us (2%)
  between operations  14.9 us (2%)
    psum x1, waiting for transfers between devices, local(): lax.psum((local_first, local_second), ('dev', 'ha'))  147 us
    transpose x3, matrix products, weight_grad(): return jnp.transpose(result, (2, 3, 4, 0, 1))  118 us
    psum x1, waiting for transfers between devices, local(): lax.psum(weight_grad(all_rows, delta_third, (0, 0), (1, 0)), 'dev')  88.5 us
    broadcast_in_dim x3, local copies, waits for them, and re-layouts, weight_grad(): inputs[:, None]  75.3 us
    psum x1, blocking collectives, local(): lax.psum((local_first, local_second), ('dev', 'ha'))  63.8 us
    all_gather x1, waiting for transfers between devices, local(): all_rows = lax.all_gather(deeper, 'ha', axis=2, tiled=True)  48 us
    conv_general_dilated x9, local copies, waits for them, and re-layouts, convolve(): lax.conv_general_dilated(inputs[None], kernel, (2, 2, 2), [pad_depth, pad...  43.6 us
    conv_general_dilated x3, matrix products, convolve(): lax.conv_general_dilated(inputs[None], kernel, (2, 2, 2), [pad_depth, pad...  38.7 us
  transfers between devices with their start and end apart: 12, of which 8 were waited for; matrix products, arithmetic and copies ran while one was open for 17% of the time, Pallas kernels for 0%

commit v1 on v0

--- a/solution.py
+++ b/solution.py
@@ -3,6 +3,11 @@
 import jax.numpy as jnp
 from jax import lax
 from jax.sharding import PartitionSpec as P
+
+
+def axis_by_axis(value, axis_one, axis_two):
+    half = lax.psum(value, axis_one)
+    return lax.psum(half, axis_two)
 
 
 def shifted(block, axis, distance):
@@ -107,7 +112,7 @@
     back_first = retract(input_grad(delta_second, w_second)[..., 1:])
     delta_first = (back_first * leaky_slope(pre_first)).astype(jnp.bfloat16)
     local_first = weight_grad(whole_first, delta_first, (0, 0), (0, 0))
-    grad_first, grad_second = lax.psum((local_first, local_second), ("dev", "ha"))
+    grad_first, grad_second = axis_by_axis((local_first, local_second), "ha", "dev")
     return (out_third, grad_first * scale_first, grad_second * scale_second, grad_third)
 
 

time: 810 us -> 710 us (0.88)
  waiting for transfers between devices: 291 us -> 152 us
  blocking collectives: 63.8 us -> 98.2 us
    psum x2, waiting for transfers between devices: 235 us -> 48.3 us  [the longest x1 48.3 us: axis_by_axis(): half = lax.psum(value, axis_one)]
    reduce_scatter x1, waiting for transfers between devices: 0.01 us -> 47.9 us  [local(): lax.psum_scatter(partial_back, 'ha', scatter_dimension=2, tiled=True)]
    psum x1 -> x2, blocking collectives: 63.8 us -> 98.2 us  [the longest x1 70.2 us: axis_by_axis(): return lax.psum(half, axis_two)]
  transfers between devices with their start and end apart: 12 -> 12, of which waited for: 8 -> 8; matrix products, arithmetic and copies ran while one was open for 17% -> 30% of each run, Pallas kernels for 0% -> 0%
where the time goes in v1:
time: 710 us; the launch traced here: 696 us
  local copies, waits for them, and re-layouts  212 us (30%)
  matrix products  168 us (24%)
  waiting for transfers between devices  152 us (21%)
  blocking collectives  98.2 us (14%)
  starting transfers between devices  32.8 us (5%)
  other arithmetic  17.6 us (2%)
  between operations  14.8 us (2%)
    transpose x3, matrix products, weight_grad(): return jnp.transpose(result, (2, 3, 4, 0, 1))  118 us
    broadcast_in_dim x3, local copies, waits for them, and re-layouts, weight_grad(): inputs[:, None]  76.3 us
    psum x1, blocking collectives, axis_by_axis(): return lax.psum(half, axis_two)  70.2 us
    psum x1, waiting for transfers between devices, axis_by_axis(): half = lax.psum(value, axis_one)  48.3 us
    all_gather x1, waiting for transfers between devices, local(): all_rows = lax.all_gather(deeper, 'ha', axis=2, tiled=True)  48 us
    reduce_scatter x1, waiting for transfers between devices, local(): lax.psum_scatter(partial_back, 'ha', scatter_dimension=2, tiled=True)  47.9 us
    conv_general_dilated x9, local copies, waits for them, and re-layouts, convolve(): lax.conv_general_dilated(inputs[None], kernel, (2, 2, 2), [pad_depth, pad...  43.5 us
    conv_general_dilated x3, matrix products, convolve(): lax.conv_general_dilated(inputs[None], kernel, (2, 2, 2), [pad_depth, pad...  38.7 us
  transfers between devices with their start and end apart: 12, of which 8 were waited for; matrix products, arithmetic and copies ran while one was open for 30% of the time, Pallas kernels for 0%

profile of v1, /device:TPU:1, one launch (start us, length us, event | category | flops | bytes accessed | tf_op | source)
XLA Modules:
  0.0 695.9 jit_solution(10084697698918230629)
XLA Ops:
  8.1 4.6 collective-permute-start
  22.9 10.8 %copy.123 = bf16[4,9,17,1,8,66]{4,0,5,2,1,3:T(4,128)(2,1)} copy(bf16[4,9,17,1,8,66]{5,4,2,1,0,3:T(8,128)(2,1)S(1)} %reshape.287) | data formatting | bytes 1292544 | tf_op jit(solution)/shard_map/conv_general_dilated | solution.py:28
  35.0 32.7 %fusion.3 = f32[4,8,8,33,32]{4,2,3,1,0:T(8,128)} fusion(bf16[3,3,3,4,32]{4,3,2,1,0:T(4,128)(2,1)S(1)} %copy-done.17, bf16[4,9,17,1,7,2]{4,0,5,2,1,3:T(4,128)(2,1)S(1)} %slice.159, bf16[4,9,17,1,8,66]{4,0,5,2,1,3:T(4,128)(2,1)} %copy.123), kind=kOutput, calls=%fused_computation.4 | convolution fusion | flops 60390144 | bytes 1751664 | tf_op jit(solution)/shard_map/conv_general_dilated | solution.py:28
  67.7 18.2 %copy.124 = f32[4,8,8,33,32]{3,4,2,1,0:T(8,128)} copy(f32[4,8,8,33,32]{4,2,3,1,0:T(8,128)} %fusion.3) | data formatting | bytes 2162688 | tf_op jit(solution)/shard_map/conv_general_dilated | solution.py:28
  85.9 5.0 select_multiply_fusion
  90.9 5.8 copy.126
  100.2 8.6 %copy.125 = f32[4,8,8,33,32]{3,2,4,1,0:T(8,128)} copy(f32[4,8,8,33,32]{3,4,2,1,0:T(8,128)} %get-tuple-element.55) | data formatting | bytes 2162688 | tf_op jit(solution)/shard_map/mul | solution.py:20
  112.9 5.1 collective-permute-start.2
  120.0 4.0 collective-permute-start.3
  131.9 4.5 copy.128
  142.8 5.2 collective-permute-start.4
  151.2 48.0 %all-gather.2.cloned.1.call-done = bf16[64,3,32,128]{3,0,1,2:T(8,128)(2,1)} async-done(((bf16[64,3,4,128]{3,0,1,2:T(8,128)(2,1)}), bf16[64,3,32,128]{3,0,1,2:T(8,128)(2,1)}) %all-gather.2.cloned.1.call-update) | async-done | bytes 1572880 | tf_op jit(solution)/shard_map/all_gather | solution.py:102
  199.2 5.8 copy.132
  212.6 4.3 broadcast_select_fusion
  216.8 5.9 copy.143
  222.7 8.9 %reshape.251 = f32[3,33,1,144,64]{4,3,1,0,2:T(8,128)} reshape(f32[3,33,8,18,64]{4,3,2,1,0:T(8,128)} %copy.143) | data formatting | bytes 7299072 | tf_op jit(solution)/shard_map/conv_general_dilated | solution.py:53
  238.8 6.2 copy.144
  245.0 47.9 %reduce-scatter.2.cloned.1.call-done = f32[64,3,4,128]{3,0,1,2:T(8,128)} async-done(((f32[64,3,32,128]{3,0,1,2:T(8,128)}), f32[64,3,4,128]{3,0,1,2:T(8,128)}) %reduce-scatter.2.cloned.1.call-update) | async-done | bytes 393232 | tf_op jit(solution)/shard_map/reduce_scatter | solution.py:108
  294.7 6.7 collective-permute-start.5
  301.5 56.9 %copy.151 = bf16[4,1,9,17,512]{0,1,4,3,2:T(2,128)(2,1)} copy(bf16[4,1,9,17,512]{4,3,2,0,1:T(8,128)(2,1)S(1)} %copy-done.10) | data formatting | bytes 1253376 | tf_op jit(solution)/shard_map/broadcast_in_dim | solution.py:40
  358.4 8.8 %copy.153 = bf16[32,1,5,9,256]{0,1,4,3,2:T(2,128)(2,1)} copy(bf16[32,1,5,9,256]{4,0,3,2,1:T(8,128)(2,1)S(1)} %copy-done.11) | data formatting | bytes 1474560 | tf_op jit(solution)/shard_map/broadcast_in_dim | solution.py:40
  368.4 10.6 %copy.156 = bf16[64,1,3,32,128]{0,1,4,3,2:T(2,128)(2,1)} copy(bf16[64,1,3,32,128]{4,0,2,3,1:T(8,128)(2,1)S(1)} %bitcast.160) | data formatting | bytes 3145728 | tf_op jit(solution)/shard_map/broadcast_in_dim | solution.py:40
  380.4 7.3 %broadcast_select_fusion.1 = f32[5,9,8,34,32]{4,2,3,1,0:T(8,128)} fusion(pred[8,34]{0,1:T(8,128)(4,1)S(1)} %copy-done.14, bf16[3,3,3,32,64]{4,3,2,1,0:T(8,128)(2,1)S(1)} %copy-done, bf16[64,2,4,1,7,1]{0,4,5,2,1,3:T(8,128)(2,1)S(1)} %slice.176, bf16[64,2,4,1,8,17]{0,4,5,2,1,3:T(8,128)(2,1)S(1)} %copy.149), kind=kOutput, calls=%fused_computation.21 | convolution fusion | flops 121158144 | bytes 1824016 | tf_op jit(solution)/shard_map/conv_general_dilated | solution.py:53
  387.8 8.3 %copy.150 = f32[5,9,8,34,32]{3,2,4,1,0:T(8,128)} copy(f32[5,9,8,34,32]{4,2,3,1,0:T(8,128)} %broadcast_select_fusion.1) | data formatting | bytes 3133440 | tf_op jit(solution)/shard_map/conv_general_dilated | solution.py:53
  396.1 4.2 reshape.258
  403.5 14.6 %fusion.35 = f32[3,3,3,32,64]{4,3,2,1,0:T(8,128)} fusion(bf16[32,1,5,9,256]{0,1,4,3,2:T(2,128)(2,1)} %copy.153, bf16[64,1,2,4,128]{0,3,4,2,1:T(4,128)(2,1)S(1)} %fusion.97), kind=kOutput, calls=%fused_computation.49 | convolution fusion | flops 112951296 | bytes 1089536 | tf_op jit(solution)/shard_map/transpose | solution.py:48
  424.6 15.3 %fusion.86 = f32[3,3,3,64,16]{3,4,2,1,0:T(8,128)} fusion(bf16[64,1,3,32,128]{0,1,4,3,2:T(2,128)(2,1)} %copy.156, bf16[16,1,1,16,64]{0,1,4,3,2:T(2,128)(2,1)} %copy.157), kind=kOutput, calls=%fused_computation.117 | convolution fusion | flops 55154688 | bytes 1716224 | tf_op jit(solution)/shard_map/transpose | solution.py:48
  440.9 48.3 %all-reduce.4.cloned.1.call-done = f32[3,3,3,32,64]{4,3,2,1,0:T(8,128)} async-done(((f32[3,3,3,32,64]{4,3,2,1,0:T(8,128)}), f32[3,3,3,32,64]{4,3,2,1,0:T(8,128)}) %all-reduce.4.cloned.1.call-update) | async-done | bytes 221200 | tf_op jit(solution)/shard_map/psum | solution.py:9
  491.6 7.3 %copy.152 = bf16[32,1,4,8,256]{0,1,4,3,2:T(2,128)(2,1)} copy(bf16[32,1,4,8,256]{4,0,3,2,1:T(8,128)(2,1)S(1)} %fusion.34) | data formatting | bytes 1048576 | tf_op jit(solution)/shard_map/broadcast_in_dim | solution.py:41
  498.9 87.7 %fusion.85 = f32[3,3,3,4,32]{4,3,2,1,0:T(4,128)S(1)} fusion(bf16[4,1,9,17,512]{0,1,4,3,2:T(2,128)(2,1)} %copy.151, bf16[32,1,4,8,256]{0,1,4,3,2:T(2,128)(2,1)} %copy.152), kind=kOutput, calls=%fused_computation.116 | convolution fusion | flops 56549376 | bytes 1164800 | tf_op jit(solution)/shard_map/transpose | solution.py:48
  586.6 28.0 %psum.35 = f32[3,3,3,4,32]{4,3,2,1,0:T(4,128)S(1)} all-reduce(f32[3,3,3,4,32]{4,3,2,1,0:T(4,128)S(1)} %fusion.85), channel_id=1, replica_groups=mesh['dev'=16,'ha'=8] {'ha'}, use_global_device_ids=true, to_apply=%region_1.2 | all-reduce | flops 3456 | bytes 27648 | tf_op jit(solution)/shard_map/psum | solution.py:9
  614.6 70.2 %psum.36 = f32[3,3,3,4,32]{4,3,2,1,0:T(4,128)S(1)} all-reduce(f32[3,3,3,4,32]{4,3,2,1,0:T(4,128)S(1)} %psum.35), channel_id=1, replica_groups=mesh['dev'=16,'ha'=8] {'dev'}, use_global_device_ids=true, to_apply=%region_2.3 | all-reduce | flops 3456 | bytes 27648 | tf_op jit(solution)/shard_map/psum | solution.py:10
  (125 shorter events, 75.3 us)
Async XLA Ops:
  7.2 130.2 %copy-start = (bf16[3,3,3,32,64]{4,3,2,1,0:T(8,128)(2,1)S(1)}, bf16[3,3,3,32,64]{4,3,2,1,0:T(8,128)(2,1)}, u32[]{:S(2)}) copy-start(bf16[3,3,3,32,64]{4,3,2,1,0:T(8,128)(2,1)} %param.13) | copy-start | bytes 331780
  7.2 192.0 %all-gather.2.cloned.1.call-start = ((), (), s32[]{:S(2)}) async-start(), calls=%async_computation.1 | async-start | bytes 1769472 | tf_op jit(solution)/shard_map/all_gather | solution.py:102
  8.1 5.9 collective-permute-start
  15.2 4.5 collective-permute-start.1
  22.9 12.0 %copy-start.17 = (bf16[3,3,3,4,32]{4,3,2,1,0:T(4,128)(2,1)S(1)}, bf16[3,3,3,4,32]{4,3,2,1,0:T(4,128)(2,1)}, u32[]{:S(2)}) copy-start(bf16[3,3,3,4,32]{4,3,2,1,0:T(4,128)(2,1)} %param.12) | copy-start | bytes 20740
  67.7 18.2 %copy-start.16 = (pred[8,33]{1,0:T(8,128)(4,1)S(1)}, pred[8,33]{1,0:T(8,128)(4,1)}, u32[]{:S(2)}) copy-start(pred[8,33]{1,0:T(8,128)(4,1)} %constant.142) | copy-start | bytes 796
  100.2 12.1 %copy-start.2 = (f32[4,8,1,264,32]{3,4,1,0,2:T(8,128)}, f32[4,8,1,264,32]{3,4,1,0,2:T(8,128)S(1)}, u32[]{:S(2)}) copy-start(f32[4,8,1,264,32]{3,4,1,0,2:T(8,128)S(1)} %reshape.226) | copy-start | bytes 3244036
  112.9 7.1 %collective-permute-start.2 = (bf16[32,1,8,256]{3,0,2,1:T(8,128)(2,1)S(1)}, bf16[32,1,8,256]{3,0,2,1:T(8,128)(2,1)S(1)}, u32[]{:S(2)}, u32[]{:S(2)}) collective-permute-start(bf16[32,1,8,256]{3,0,2,1:T(8,128)(2,1)S(1)} %slice.162), channel_id=1, source_target_pairs={{0,8},{8,16},{16,24},{24,32},{32,40},{40,48},{48,56},{56,64},{64,7... | collective-permute-start | bytes 393224 | tf_op jit(solution)/shard_map/ppermute | solution.py:16
  120.0 5.5 collective-permute-start.3
  131.9 5.5 copy-start.18
  142.8 7.1 %collective-permute-start.4 = (bf16[64,1,4,128]{0,2,3,1:T(4,128)(2,1)S(1)}, bf16[64,1,4,128]{0,2,3,1:T(4,128)(2,1)S(1)}, u32[]{:S(2)}, u32[]{:S(2)}) collective-permute-start(bf16[64,1,4,128]{0,2,3,1:T(4,128)(2,1)S(1)} %slice.166), channel_id=1, source_target_pairs={{0,8},{8,16},{16,24},{24,32},{32,40},{40,48},{48,56},{56,64},{64,7... | collective-permute-start | bytes 196616 | tf_op jit(solution)/shard_map/ppermute | solution.py:16
  151.2 141.7 %reduce-scatter.2.cloned.1.call-start = ((), (), s32[]{:S(2)}) async-start(), calls=%async_computation.2 | async-start | bytes 3538944 | tf_op jit(solution)/shard_map/reduce_scatter | solution.py:108
  205.6 2.4 copy-start.12
  205.6 2.4 copy-start.19
  210.3 0.9 copy-start.13
  210.3 2.2 copy-start.15
  245.0 56.5 %copy-start.10 = (bf16[4,1,9,17,512]{4,3,2,0,1:T(8,128)(2,1)S(1)}, bf16[4,1,9,17,512]{4,3,2,0,1:T(8,128)(2,1)}, u32[]{:S(2)}) copy-start(bf16[4,1,9,17,512]{4,3,2,0,1:T(8,128)(2,1)} %get-tuple-element.58) | copy-start | bytes 1880068
  245.0 244.3 %all-reduce.4.cloned.1.call-start = ((), (), s32[]{:S(2)}) async-start(), calls=%async_computation.3 | async-start | bytes 884736 | tf_op jit(solution)/shard_map/psum | solution.py:9
  294.7 84.6 %collective-permute-start.5 = (f32[64,1,4,128]{0,2,3,1:T(4,128)}, f32[64,1,4,128]{0,2,3,1:T(4,128)S(1)}, u32[]{:S(2)}, u32[]{:S(2)}) collective-permute-start(f32[64,1,4,128]{0,2,3,1:T(4,128)} %copy.168), channel_id=1, source_target_pairs={{8,0},{16,8},{24,16},{32,24},{40,32},{48,40},{56,48},{64,56},{72,6... | collective-permute-start | bytes 393224 | tf_op jit(solution)/shard_map/ppermute | solution.py:16
  301.5 56.9 %copy-start.11 = (bf16[32,1,5,9,256]{4,0,3,2,1:T(8,128)(2,1)S(1)}, bf16[32,1,5,9,256]{4,0,3,2,1:T(8,128)(2,1)}, u32[]{:S(2)}) copy-start(bf16[32,1,5,9,256]{4,0,3,2,1:T(8,128)(2,1)} %get-tuple-element.56) | copy-start | bytes 2211844
  358.4 10.0 %copy-start.9 = (bf16[64,3,32,128]{3,0,1,2:T(8,128)(2,1)S(1)}, bf16[64,3,32,128]{3,0,1,2:T(8,128)(2,1)}, u32[]{:S(2)}) copy-start(bf16[64,3,32,128]{3,0,1,2:T(8,128)(2,1)} %all-gather.2.cloned.1.call-done) | copy-start | bytes 4718596
  368.4 10.8 %slice-start = ((f32[64,3,4,128]{3,0,1,2:T(8,128)}), f32[64,2,4,128]{3,0,1,2:T(8,128)S(1)}, s32[]{:S(2)}) async-start(f32[64,3,4,128]{3,0,1,2:T(8,128)} %reduce-scatter.2.cloned.1.call-done), calls=%async_computation.5 | async-start | bytes 524288 | tf_op jit(solution)/shard_map/slice | solution.py:77
  368.4 11.1 %copy-start.5 = (f32[2,4,8,17,64]{4,1,3,2,0:T(4,128)S(1)}, f32[2,4,8,17,64]{4,1,3,2,0:T(4,128)}, u32[]{:S(2)}) copy-start(f32[2,4,8,17,64]{4,1,3,2,0:T(4,128)} %copy-done.4) | copy-start | bytes 835588
  379.0 1.5 copy-start.14
  400.4 1.4 copy-start.6
  401.9 16.3 %copy-start.7 = (f32[32,5,9,257]{3,0,2,1:T(8,128)S(1)}, f32[32,5,9,257]{3,0,2,1:T(8,128)}, u32[]{:S(2)}) copy-start(f32[32,5,9,257]{3,0,2,1:T(8,128)} %copy-done.6) | copy-start | bytes 4440964
  401.9 17.9 %collective-permute-start.6 = (bf16[32,5,1,256]{3,0,2,1:T(8,128)(2,1)S(1)}, bf16[32,5,1,256]{3,0,2,1:T(8,128)(2,1)S(1)}, u32[]{:S(2)}, u32[]{:S(2)}) collective-permute-start(bf16[32,5,1,256]{3,0,2,1:T(8,128)(2,1)S(1)} %slice.211), channel_id=1, source_target_pairs={{1,0},{2,1},{3,2},{4,3},{5,4},{6,5},{7,6},{9,8},{10,9},{11,10},{12... | collective-permute-start | bytes 245768 | tf_op jit(solution)/shard_map/ppermute | solution.py:16
  419.7 265.7 %all-reduce.6.cloned.1.call-start = ((), (), s32[]{:S(2)}) async-start(), calls=%async_computation.4 | async-start | bytes 1327104 | tf_op jit(solution)/shard_map/psum | solution.py:10
  422.3 17.6 %copy-start.8 = (f32[32,5,8,256]{3,0,2,1:T(8,128)S(1)}, f32[32,5,8,256]{3,0,2,1:T(8,128)}, u32[]{:S(2)}) copy-start(f32[32,5,8,256]{3,0,2,1:T(8,128)} %fusion.52) | copy-start | bytes 3932164
  422.3 67.0 %collective-permute-start.7 = (f32[32,1,8,256]{3,0,2,1:T(8,128)}, f32[32,1,8,256]{3,0,2,1:T(8,128)S(1)}, u32[]{:S(2)}, u32[]{:S(2)}) collective-permute-start(f32[32,1,8,256]{3,0,2,1:T(8,128)} %slice.183), channel_id=1, source_target_pairs={{8,0},{16,8},{24,16},{32,24},{40,32},{48,40},{56,48},{64,56},{72,6... | collective-permute-start | bytes 786440 | tf_op jit(solution)/shard_map/ppermute | solution.py:16
  439.9 50.2 %copy-start.3 = (f32[4,8,1,264,32]{3,4,1,0,2:T(8,128)S(1)}, f32[4,8,1,264,32]{3,4,1,0,2:T(8,128)}, u32[]{:S(2)}) copy-start(f32[4,8,1,264,32]{3,4,1,0,2:T(8,128)} %copy-done.2) | copy-start | bytes 3244036
  498.9 190.0 %copy-start.1 = (bf16[3,3,3,32,64]{4,3,2,1,0:T(8,128)(2,1)S(1)}, bf16[3,3,3,32,64]{4,3,2,1,0:T(8,128)(2,1)}, u32[]{:S(2)}) copy-start(bf16[3,3,3,32,64]{4,3,2,1,0:T(8,128)(2,1)} %param.13) | copy-start | bytes 331780
  (1 other events, 0.8 us)
Sparse Core Ops, SparseCore 0:
  151.3 47.8 all-gather.1
  245.1 47.7 reduce-scatter.1
  419.8 69.3 all-reduce.3
  492.2 142.0 all-reduce.5
